TPU v7x, 32 devices: a whole 2x2x4 slice. The times are simulated.
32 devices in a mesh: obs: 4 (over y, core), flux: 8 (over z, x).
Axes of the slice: x: 2, y: 2, z: 4, core: 2. Of those that a mesh axis runs over, the one named last changes fastest.
Arguments:
- jacobian: bfloat16 [512, 8192], P('obs', 'flux'), may hold values from -0.0625 to 0.0625
- probes: bfloat16 [2, 8192, 128], P(None, 'flux'), may hold values from -6 to 6
- prior_std: float32 [8192], P('flux'), may hold values from 0.5 to 2
- obs_weight: float32 [512], P('obs'), may hold values from 0.25 to 4
Outputs:
- sketch: float32 [8192, 256], P(('flux', 'obs'))
- basis_out: float32 [8192, 256], P(('flux', 'obs'))
All inputs are finite; a program needn't handle non-finite values.
Results may differ from a plain program's by a relative error of at most 0.005.
Values may be sent and summed in bfloat16 or wider, within the bound.
A program may use at most 64 MiB of HBM per device.

v0:
```python
import math
import jax
import jax.numpy as jnp
from jax import lax
from jax.sharding import PartitionSpec as P


def body(jacobian, probes, prior_std, obs_weight):
    block_count, flux_local, probe_count = probes.shape
    scaled = (probes.astype(jnp.float32) * prior_std[None, :, None]).astype(jnp.bfloat16)
    portion = flux_local // lax.axis_size("obs")
    offset = lax.axis_index("obs") * portion
    local_std = lax.dynamic_slice_in_dim(prior_std, offset, portion)
    stacked = jnp.transpose(scaled, (1, 0, 2)).reshape(flux_local, block_count * probe_count)
    forward = lax.psum(jnp.dot(jacobian, stacked, preferred_element_type=jnp.float32), "flux")
    weighted = (forward * obs_weight[:, None]).astype(jnp.bfloat16)
    adjoint = lax.psum_scatter(
        lax.dot_general(
            jacobian, weighted, (((0,), (0,)), ((), ())), preferred_element_type=jnp.float32
        ),
        "obs",
        scatter_dimension=0,
        tiled=True,
    )
    sketch = adjoint * local_std[:, None]
    gram_matrix = lax.psum(
        jnp.dot(
            sketch.T, sketch, precision=lax.Precision.HIGHEST, preferred_element_type=jnp.float32
        ),
        ("obs", "flux"),
    )
    factor = jnp.linalg.cholesky(gram_matrix)
    scale_root = math.sqrt(flux_local * lax.axis_size("flux"))
    basis_out = jax.scipy.linalg.solve_triangular(factor, sketch.T, lower=True).T * scale_root
    return (sketch, basis_out)


def solution(mesh):
    in_specs = (P("obs", "flux"), P(None, "flux", None), P("flux"), P("obs"))
    out_specs = (P(("flux", "obs"), None), P(("flux", "obs"), None))
    return jax.shard_map(body, mesh=mesh, in_specs=in_specs, out_specs=out_specs, check_vma=False)
```

profile of v0, /device:TPU:0, one launch (start us, length us, event | category | flops | bytes accessed | tf_op | source)
XLA Modules:
  0.0 313.9 jit_solution(5051485426730443432)
XLA Ops:
  7.2 1.3 copy.10
  8.7 1.0 convolution_bitcast_fusion.1
  9.7 75.5 %all-reduce.4.cloned.1.call-done = f32[128,256]{0,1:T(8,128)} async-done(((f32[128,256]{0,1:T(8,128)}), f32[128,256]{0,1:T(8,128)}) %all-reduce.4.cloned.1.call-update) | async-done | bytes 131088 | tf_op jit(solution)/shard_map/psum | solution.py:15
  85.2 2.2 convolution_bitcast_fusion
  87.5 24.1 %reduce-scatter.2.cloned.1.call-done = f32[256,256]{0,1:T(8,128)} async-done(((f32[1024,256]{0,1:T(8,128)}), f32[256,256]{0,1:T(8,128)}) %reduce-scatter.2.cloned.1.call-update) | async-done | bytes 262160 | tf_op jit(solution)/shard_map/reduce_scatter | solution.py:17
  111.6 1.0 broadcast_multiply_fusion
  112.6 0.8 copy.13
  113.4 1.1 fusion.11
  114.6 0.9 copy-done.2
  115.5 128.9 %all-reduce.6.cloned.1.call-done = f32[256,256]{0,1:T(8,128)} async-done(((f32[256,256]{0,1:T(8,128)}), f32[256,256]{0,1:T(8,128)}) %all-reduce.6.cloned.1.call-update) | async-done | bytes 262160 | tf_op jit(solution)/shard_map/psum | solution.py:26
  244.4 1.1 copy.12
  245.6 11.7 %cholesky.50 = f32[128,128]{1,0:T(8,128)S(1)} custom-call(f32[128,128]{1,0:T(8,128)S(1)} %cholesky.118), custom_call_target="Cholesky" | custom-call | tf_op jit(solution)/shard_map/jit(cholesky)/cholesky | solution.py:32
  257.4 9.8 %custom-call.15 = f32[1,128,128]{1,2,0:T(8,128)S(1)} custom-call(f32[1,128,128]{2,1,0:T(8,128)S(1)} %get-tuple-element.27), custom_call_target="InvertDiagBlocksLowerTriangular" | custom-call | tf_op jit(solution)/shard_map/jit(cholesky)/cholesky | solution.py:32
  267.7 11.7 %cholesky.105 = f32[128,128]{1,0:T(8,128)S(1)} custom-call(f32[128,128]{1,0:T(8,128)S(1)} %convolution_subtract_fusion.1), custom_call_target="Cholesky" | custom-call | tf_op jit(solution)/shard_map/jit(cholesky)/cholesky | solution.py:32
  279.5 0.7 compare_reduce_fusion
  281.6 4.2 %while.1 = (s32[]{:T(128)}, f32[256,256]{1,0:T(8,128)S(1)}, s32[2,2]{1,0:T(2,128)S(1)}, f32[2,128,128]{2,1,0:T(8,128)S(1)}, s32[]{:T(128)}) while((s32[]{:T(128)}, f32[256,256]{1,0:T(8,128)S(1)}, s32[2,2]{1,0:T(2,128)S(1)}, f32[2,128,128]{2,1,0:T(8,128)S(1)}, s32[]{:T(128)}) %tuple.29), condition=%wide.while_cond, body=%wide.while_body.sunk | while | flops 2 | bytes 131189 | solution.py:34
  281.8 0.6 fusion.23
  282.4 1.4 bitcast_dynamic-update-slice_fusion.2
  283.8 0.6 fusion.23
  284.4 1.4 bitcast_dynamic-update-slice_fusion.2
  285.9 19.7 %custom-call.16 = f32[2,128,128]{1,2,0:T(8,128)S(1)} custom-call(f32[2,128,128]{2,1,0:T(8,128)S(1)} %get-tuple-element.9), custom_call_target="InvertDiagBlocksLowerTriangular" | custom-call | tf_op jit(solution)/shard_map/jit(_solve_triangular)/triangular_solve | solution.py:34
  305.6 0.3 fusion.2
  306.1 0.3 fusion.5
  306.5 0.8 copy.14
  (33 shorter events, 1.4 us)
Async XLA Ops:
  7.2 1.5 copy-start
  7.2 1.3 copy-start.3
  7.2 78.0 %all-reduce.4.cloned.1.call-start = ((), (), s32[]{:S(2)}) async-start(), calls=%async_computation.1 | async-start | bytes 262144 | tf_op jit(solution)/shard_map/psum | solution.py:15
  9.6 75.6 %copy-start.4 = (f32[128]{0:T(128)S(1)}, f32[128]{0:T(128)}, u32[]{:S(2)}) copy-start(f32[128]{0:T(128)} %param.7) | copy-start | bytes 1540
  9.6 102.0 %reduce-scatter.2.cloned.1.call-start = ((), (), s32[]{:S(2)}) async-start(), calls=%async_computation.2 | async-start | bytes 1310720 | tf_op jit(solution)/shard_map/reduce_scatter | solution.py:17
  87.4 157.0 %all-reduce.6.cloned.1.call-start = ((), (), s32[]{:S(2)}) async-start(), calls=%async_computation.3 | async-start | bytes 524288 | tf_op jit(solution)/shard_map/psum | solution.py:26
  114.6 0.9 copy-start.2
  244.4 1.2 copy-start.1
Sparse Core Ops, SparseCore 0:
  11.9 73.2 all-reduce.3
  87.7 23.8 reduce-scatter.1
  117.7 126.6 all-reduce.5
where the time goes:
time: 314 us
  waiting for transfers between devices  229 us (73%)
  other arithmetic  54.9 us (17%)
  between operations  15.3 us (5%)
  local copies, waits for them, and re-layouts  9.28 us (3%)
  matrix products  5.61 us (2%)
    psum x1, waiting for transfers between devices, body(): lax.psum(jnp.dot(sketch.T, sketch, precision=lax.Precision.HIGHEST, prefe...  129 us
    psum x1, waiting for transfers between devices, body(): lax.psum(jnp.dot(jacobian, stacked, preferred_element_type=jnp.float32),...  75.5 us
    another operation x6, other arithmetic, body(): factor = jnp.linalg.cholesky(gram_matrix)  34 us
    reduce_scatter x1, waiting for transfers between devices, body(): lax.psum_scatter(lax.dot_general(jacobian, weighted, (((0,), (0,)), ((),...  24.1 us
    another operation x3, other arithmetic, body(): jax.scipy.linalg.solve_triangular(factor, sketch.T, lower=True)  19.7 us
  transfers between devices with their start and end apart: 3, of which 3 were waited for; matrix products, arithmetic and copies ran while one was open for 0% of the time, Pallas kernels for 0%

commit v1 on v0

--- a/solution.py
+++ b/solution.py
@@ -24,10 +24,16 @@
     )
     sketch = adjoint * local_std[:, None]
     gram_matrix = lax.psum(
-        jnp.dot(
-            sketch.T, sketch, precision=lax.Precision.HIGHEST, preferred_element_type=jnp.float32
+        lax.psum(
+            jnp.dot(
+                sketch.T,
+                sketch,
+                precision=lax.Precision.HIGHEST,
+                preferred_element_type=jnp.float32,
+            ),
+            "flux",
         ),
-        ("obs", "flux"),
+        "obs",
     )
     factor = jnp.linalg.cholesky(gram_matrix)
     scale_root = math.sqrt(flux_local * lax.axis_size("flux"))

time: 314 us -> 290 us (0.924)
  waiting for transfers between devices: 229 us -> 205 us
    psum x1, waiting for transfers between devices: 129 us -> 72 us  [body(): lax.psum(jnp.dot(sketch.T, sketch, precision=lax.Precision.HIGHEST, prefe...]
    psum x0 -> x1, waiting for transfers between devices: none -> 33.6 us  [body(): lax.psum(lax.psum(jnp.dot(sketch.T, sketch, precision=lax.Precision.HIGHE...]
  transfers between devices with their start and end apart: 3 -> 4, of which waited for: 3 -> 4; matrix products, arithmetic and copies ran while one was open for 0% -> 0% of each run, Pallas kernels for 0% -> 0%
where the time goes in v1:
time: 290 us
  waiting for transfers between devices  205 us (71%)
  other arithmetic  54.9 us (19%)
  between operations  15.3 us (5%)
  local copies, waits for them, and re-layouts  8.36 us (3%)
  matrix products  5.61 us (2%)
    psum x1, waiting for transfers between devices, body(): lax.psum(jnp.dot(jacobian, stacked, preferred_element_type=jnp.float32),...  75.5 us
    psum x1, waiting for transfers between devices, body(): lax.psum(jnp.dot(sketch.T, sketch, precision=lax.Precision.HIGHEST, prefe...  72 us
    another operation x6, other arithmetic, body(): factor = jnp.linalg.cholesky(gram_matrix)  34 us
    psum x1, waiting for transfers between devices, body(): lax.psum(lax.psum(jnp.dot(sketch.T, sketch, precision=lax.Precision.HIGHE...  33.6 us
    reduce_scatter x1, waiting for transfers between devices, body(): lax.psum_scatter(lax.dot_general(jacobian, weighted, (((0,), (0,)), ((),...  24.1 us
    another operation x3, other arithmetic, body(): jax.scipy.linalg.solve_triangular(factor, sketch.T, lower=True)  19.7 us
  transfers between devices with their start and end apart: 4, of which 4 were waited for; matrix products, arithmetic and copies ran while one was open for 0% of the time, Pallas kernels for 0%

profile of v1, /device:TPU:0, one launch (start us, length us, event | category | flops | bytes accessed | tf_op | source)
XLA Modules:
  0.0 289.8 jit_solution(7751516162686516787)
XLA Ops:
  7.2 1.3 copy.10
  8.7 1.0 convolution_bitcast_fusion.1
  9.7 75.5 %all-reduce.5.cloned.1.call-done = f32[128,256]{0,1:T(8,128)} async-done(((f32[128,256]{0,1:T(8,128)}), f32[128,256]{0,1:T(8,128)}) %all-reduce.5.cloned.1.call-update) | async-done | bytes 131088 | tf_op jit(solution)/shard_map/psum | solution.py:15
  85.2 2.2 convolution_bitcast_fusion
  87.5 24.1 %reduce-scatter.2.cloned.1.call-done = f32[256,256]{0,1:T(8,128)} async-done(((f32[1024,256]{0,1:T(8,128)}), f32[256,256]{0,1:T(8,128)}) %reduce-scatter.2.cloned.1.call-update) | async-done | bytes 262160 | tf_op jit(solution)/shard_map/reduce_scatter | solution.py:17
  111.6 1.0 broadcast_multiply_fusion
  112.6 1.1 fusion.11
  113.8 0.8 copy.13
  114.7 72.0 %all-reduce.7.cloned.1.call-done = f32[256,256]{0,1:T(8,128)} async-done(((f32[256,256]{0,1:T(8,128)}), f32[256,256]{0,1:T(8,128)}) %all-reduce.7.cloned.1.call-update) | async-done | bytes 262160 | tf_op jit(solution)/shard_map/psum | solution.py:27
  186.7 33.6 %all-reduce.9.cloned.1.call-done = f32[256,256]{0,1:T(8,128)} async-done(((f32[256,256]{0,1:T(8,128)}), f32[256,256]{0,1:T(8,128)}) %all-reduce.9.cloned.1.call-update) | async-done | bytes 262160 | tf_op jit(solution)/shard_map/psum | solution.py:26
  220.3 1.1 copy.12
  221.6 11.7 %cholesky.50 = f32[128,128]{1,0:T(8,128)S(1)} custom-call(f32[128,128]{1,0:T(8,128)S(1)} %cholesky.118), custom_call_target="Cholesky" | custom-call | tf_op jit(solution)/shard_map/jit(cholesky)/cholesky | solution.py:38
  233.3 9.8 %custom-call.15 = f32[1,128,128]{1,2,0:T(8,128)S(1)} custom-call(f32[1,128,128]{2,1,0:T(8,128)S(1)} %get-tuple-element.27), custom_call_target="InvertDiagBlocksLowerTriangular" | custom-call | tf_op jit(solution)/shard_map/jit(cholesky)/cholesky | solution.py:38
  243.6 11.7 %cholesky.105 = f32[128,128]{1,0:T(8,128)S(1)} custom-call(f32[128,128]{1,0:T(8,128)S(1)} %convolution_subtract_fusion.1), custom_call_target="Cholesky" | custom-call | tf_op jit(solution)/shard_map/jit(cholesky)/cholesky | solution.py:38
  255.4 0.7 compare_reduce_fusion
  257.5 4.2 %while.1 = (s32[]{:T(128)}, f32[256,256]{1,0:T(8,128)S(1)}, s32[2,2]{1,0:T(2,128)S(1)}, f32[2,128,128]{2,1,0:T(8,128)S(1)}, s32[]{:T(128)}) while((s32[]{:T(128)}, f32[256,256]{1,0:T(8,128)S(1)}, s32[2,2]{1,0:T(2,128)S(1)}, f32[2,128,128]{2,1,0:T(8,128)S(1)}, s32[]{:T(128)}) %tuple.29), condition=%wide.while_cond, body=%wide.while_body.sunk | while | flops 2 | bytes 131189 | solution.py:40
  257.7 0.6 fusion.23
  258.3 1.4 bitcast_dynamic-update-slice_fusion.2
  259.8 0.6 fusion.23
  260.3 1.4 bitcast_dynamic-update-slice_fusion.2
  261.8 19.7 %custom-call.16 = f32[2,128,128]{1,2,0:T(8,128)S(1)} custom-call(f32[2,128,128]{2,1,0:T(8,128)S(1)} %get-tuple-element.9), custom_call_target="InvertDiagBlocksLowerTriangular" | custom-call | tf_op jit(solution)/shard_map/jit(_solve_triangular)/triangular_solve | solution.py:40
  281.5 0.3 fusion.2
  282.1 0.3 fusion.5
  282.4 0.8 copy.14
  (36 shorter events, 1.5 us)
Async XLA Ops:
  7.2 1.5 copy-start
  7.2 1.3 copy-start.3
  7.2 78.0 %all-reduce.5.cloned.1.call-start = ((), (), s32[]{:S(2)}) async-start(), calls=%async_computation.1 | async-start | bytes 262144 | tf_op jit(solution)/shard_map/psum | solution.py:15
  9.6 75.6 %copy-start.4 = (f32[128]{0:T(128)S(1)}, f32[128]{0:T(128)}, u32[]{:S(2)}) copy-start(f32[128]{0:T(128)} %param.7) | copy-start | bytes 1540
  9.6 102.0 %reduce-scatter.2.cloned.1.call-start = ((), (), s32[]{:S(2)}) async-start(), calls=%async_computation.2 | async-start | bytes 1310720 | tf_op jit(solution)/shard_map/reduce_scatter | solution.py:17
  87.4 99.2 %all-reduce.7.cloned.1.call-start = ((), (), s32[]{:S(2)}) async-start(), calls=%async_computation.3 | async-start | bytes 524288 | tf_op jit(solution)/shard_map/psum | solution.py:27
  113.7 106.6 %all-reduce.9.cloned.1.call-start = ((), (), s32[]{:S(2)}) async-start(), calls=%async_computation.4 | async-start | bytes 524288 | tf_op jit(solution)/shard_map/psum | solution.py:26
  114.7 72.0 %copy-start.2 = (f32[256,256]{0,1:T(8,128)S(1)}, f32[256,256]{0,1:T(8,128)}, u32[]{:S(2)}) copy-start(f32[256,256]{0,1:T(8,128)} %reduce-scatter.2.cloned.1.call-done) | copy-start | bytes 786436
  220.3 1.2 copy-start.1
Sparse Core Ops, SparseCore 0:
  11.9 73.2 all-reduce.4
  87.7 23.8 reduce-scatter.1
  115.6 71.0 all-reduce.6
  188.8 31.4 all-reduce.8

commit v2 on v0

--- a/solution.py
+++ b/solution.py
@@ -23,11 +23,17 @@
         tiled=True,
     )
     sketch = adjoint * local_std[:, None]
-    gram_matrix = lax.psum(
-        jnp.dot(
-            sketch.T, sketch, precision=lax.Precision.HIGHEST, preferred_element_type=jnp.float32
+    gram_matrix = jnp.sum(
+        lax.all_gather(
+            jnp.dot(
+                sketch.T,
+                sketch,
+                precision=lax.Precision.HIGHEST,
+                preferred_element_type=jnp.float32,
+            ),
+            ("obs", "flux"),
         ),
-        ("obs", "flux"),
+        axis=0,
     )
     factor = jnp.linalg.cholesky(gram_matrix)
     scale_root = math.sqrt(flux_local * lax.axis_size("flux"))

time: 314 us -> 265 us (0.84)
  waiting for transfers between devices: 229 us -> 175 us
  other arithmetic: 54.9 us -> 60.5 us
    psum x1 -> x0, waiting for transfers between devices: 129 us -> none  [body(): lax.psum(jnp.dot(sketch.T, sketch, precision=lax.Precision.HIGHEST, prefe...]
    all_gather x0 -> x1, waiting for transfers between devices: none -> 76.8 us  [body(): lax.all_gather(jnp.dot(sketch.T, sketch, precision=lax.Precision.HIGHEST,...]
    reduce_sum x0 -> x1, other arithmetic: none -> 3.93 us  [body(): jnp.sum(lax.all_gather(jnp.dot(sketch.T, sketch, precision=lax.Precision....]
  transfers between devices with their start and end apart: 3 -> 3, of which waited for: 3 -> 3; matrix products, arithmetic and copies ran while one was open for 0% -> 1% of each run, Pallas kernels for 0% -> 0%
where the time goes in v2:
time: 265 us
  waiting for transfers between devices  175 us (66%)
  other arithmetic  60.5 us (23%)
  between operations  15.2 us (6%)
  local copies, waits for them, and re-layouts  8.01 us (3%)
  matrix products  5.62 us (2%)
    all_gather x1, waiting for transfers between devices, body(): lax.all_gather(jnp.dot(sketch.T, sketch, precision=lax.Precision.HIGHEST,...  76.8 us
    psum x1, waiting for transfers between devices, body(): lax.psum(jnp.dot(jacobian, stacked, preferred_element_type=jnp.float32),...  74.8 us
    another operation x6, other arithmetic, body(): factor = jnp.linalg.cholesky(gram_matrix)  34 us
    reduce_scatter x1, waiting for transfers between devices, body(): lax.psum_scatter(lax.dot_general(jacobian, weighted, (((0,), (0,)), ((),...  23.4 us
    another operation x3, other arithmetic, body(): jax.scipy.linalg.solve_triangular(factor, sketch.T, lower=True)  19.7 us
  transfers between devices with their start and end apart: 3, of which 3 were waited for; matrix products, arithmetic and copies ran while one was open for 1% of the time, Pallas kernels for 0%

profile of v2, /device:TPU:0, one launch (start us, length us, event | category | flops | bytes accessed | tf_op | source)
XLA Modules:
  0.0 264.7 jit_solution(13453754090607849242)
XLA Ops:
  7.2 1.3 copy.13
  8.5 0.8 multiply_convert_fusion
  9.3 1.0 convolution_bitcast_fusion.1
  10.4 74.8 %all-reduce.3.cloned.1.call-done = f32[128,256]{0,1:T(8,128)} async-done(((f32[128,256]{0,1:T(8,128)}), f32[128,256]{0,1:T(8,128)}) %all-reduce.3.cloned.1.call-update) | async-done | bytes 131088 | tf_op jit(solution)/shard_map/psum | solution.py:15
  85.2 2.2 convolution_bitcast_fusion
  87.4 0.8 dynamic_slice.3
  88.2 23.4 %reduce-scatter.2.cloned.1.call-done = f32[256,256]{0,1:T(8,128)} async-done(((f32[1024,256]{0,1:T(8,128)}), f32[256,256]{0,1:T(8,128)}) %reduce-scatter.2.cloned.1.call-update) | async-done | bytes 262160 | tf_op jit(solution)/shard_map/reduce_scatter | solution.py:17
  111.6 1.0 broadcast_multiply_fusion
  112.6 1.1 fusion.11
  113.8 0.8 copy.15
  114.6 1.0 fusion.21
  115.6 76.8 %all-gather.3.cloned.1.call-done = f32[8192,256]{1,0:T(8,128)} async-done(((f32[256,256]{1,0:T(8,128)}), f32[8192,256]{1,0:T(8,128)}) %all-gather.3.cloned.1.call-update) | async-done | bytes 8388624 | tf_op jit(solution)/shard_map/all_gather | solution.py:27
  192.3 3.9 %reduce_sum.9 = f32[256,256]{1,0:T(8,128)S(1)} reduce(f32[32,256,256]{2,1,0:T(8,128)} %bitcast.48, f32[]{:T(128)} %constant.87.clone.1), dimensions={0}, to_apply=%region_2.0 | reduce | flops 2031616 | bytes 8650756 | tf_op jit(solution)/shard_map/reduce_sum | solution.py:26
  196.5 11.7 %cholesky.50 = f32[128,128]{1,0:T(8,128)S(1)} custom-call(f32[128,128]{1,0:T(8,128)S(1)} %cholesky.118), custom_call_target="Cholesky" | custom-call | tf_op jit(solution)/shard_map/jit(cholesky)/cholesky | solution.py:38
  208.2 9.8 %custom-call.15 = f32[1,128,128]{1,2,0:T(8,128)S(1)} custom-call(f32[1,128,128]{2,1,0:T(8,128)S(1)} %get-tuple-element.29), custom_call_target="InvertDiagBlocksLowerTriangular" | custom-call | tf_op jit(solution)/shard_map/jit(cholesky)/cholesky | solution.py:38
  218.5 11.7 %cholesky.105 = f32[128,128]{1,0:T(8,128)S(1)} custom-call(f32[128,128]{1,0:T(8,128)S(1)} %convolution_subtract_fusion.1), custom_call_target="Cholesky" | custom-call | tf_op jit(solution)/shard_map/jit(cholesky)/cholesky | solution.py:38
  230.3 0.7 compare_reduce_fusion
  232.4 4.2 %while.1 = (s32[]{:T(128)}, f32[256,256]{1,0:T(8,128)S(1)}, s32[2,2]{1,0:T(2,128)S(1)}, f32[2,128,128]{2,1,0:T(8,128)S(1)}, s32[]{:T(128)}) while((s32[]{:T(128)}, f32[256,256]{1,0:T(8,128)S(1)}, s32[2,2]{1,0:T(2,128)S(1)}, f32[2,128,128]{2,1,0:T(8,128)S(1)}, s32[]{:T(128)}) %tuple.30), condition=%wide.while_cond, body=%wide.while_body.sunk | while | flops 2 | bytes 131189 | solution.py:40
  232.6 0.6 fusion.23
  233.2 1.4 bitcast_dynamic-update-slice_fusion.2
  234.7 0.6 fusion.23
  235.2 1.4 bitcast_dynamic-update-slice_fusion.2
  236.7 19.7 %custom-call.16 = f32[2,128,128]{1,2,0:T(8,128)S(1)} custom-call(f32[2,128,128]{2,1,0:T(8,128)S(1)} %get-tuple-element.9), custom_call_target="InvertDiagBlocksLowerTriangular" | custom-call | tf_op jit(solution)/shard_map/jit(_solve_triangular)/triangular_solve | solution.py:40
  257.3 0.8 copy.16
  (26 shorter events, 1.9 us)
Async XLA Ops:
  7.2 2.1 copy-start
  7.2 78.0 %all-reduce.3.cloned.1.call-start = ((), (), s32[]{:S(2)}) async-start(), calls=%async_computation.1 | async-start | bytes 262144 | tf_op jit(solution)/shard_map/psum | solution.py:15
  10.3 101.3 %reduce-scatter.2.cloned.1.call-start = ((), (), s32[]{:S(2)}) async-start(), calls=%async_computation.2 | async-start | bytes 1310720 | tf_op jit(solution)/shard_map/reduce_scatter | solution.py:17
  87.4 104.9 %all-gather.3.cloned.1.call-start = ((), (), s32[]{:S(2)}) async-start(), calls=%async_computation.3 | async-start | bytes 8650752 | tf_op jit(solution)/shard_map/all_gather | solution.py:27
Sparse Core Ops, SparseCore 0:
  11.9 73.2 all-reduce.2
  87.7 23.8 reduce-scatter.1
  115.2 77.0 all-gather.2
